TPU v7x, 32 devices: a whole 2x2x4 slice. The times are simulated.
32 devices in a mesh: dp: 4 (over z), fsdp: 8 (over y, x, core).
Axes of the slice: x: 2, y: 2, z: 4, core: 2. Of those that a mesh axis runs over, the one named last changes fastest.
Arguments:
- tokens: bfloat16 [4096, 2048], P(('dp', 'fsdp')), may hold values from -6 to 6
- ln_gain: float32 [2048], replicated, may hold values from 0.5 to 1.5
- ln_shift: float32 [2048], replicated, may hold values from -3 to 3
- w_qkv: bfloat16 [2048, 6144], P(('dp', 'fsdp')), may hold values from -0.125 to 0.125
- b_qkv: float32 [6144], replicated, may hold values from -3 to 3
- w_out: bfloat16 [2048, 2048], P(('dp', 'fsdp')), may hold values from -0.5 to 0.5
- w_gate: bfloat16 [2048, 5632], P(('dp', 'fsdp')), may hold values from -0.125 to 0.125
- w_up: bfloat16 [2048, 5632], P(('dp', 'fsdp')), may hold values from -0.125 to 0.125
- w_down: bfloat16 [5632, 2048], P(('dp', 'fsdp')), may hold values from -0.078125 to 0.078125
- grad_out: bfloat16 [4096, 2048], P(('dp', 'fsdp')), may hold values from -6 to 6
- seq_lengths: int32 [32, 4], P(('dp', 'fsdp')), may hold values from 0 to 128, as said below
Outputs:
- output: bfloat16 [4096, 2048], P(('dp', 'fsdp'))
- grad_tokens: bfloat16 [4096, 2048], P(('dp', 'fsdp'))
- grad_w_qkv: float32 [2048, 6144], P(('dp', 'fsdp'))
- grad_w_out: float32 [2048, 2048], P(('dp', 'fsdp'))
- grad_w_gate: float32 [2048, 5632], P(('dp', 'fsdp'))
- grad_w_up: float32 [2048, 5632], P(('dp', 'fsdp'))
- grad_w_down: float32 [5632, 2048], P(('dp', 'fsdp'))
- grad_gain: float32 [2048], P(('dp', 'fsdp'))
- grad_shift: float32 [2048], P(('dp', 'fsdp'))
- grad_bias: float32 [6144], P(('dp', 'fsdp'))
Inputs may be any that keep to these rules, and one draw needn't show every extreme that they name: `seq_lengths`: each device's row of lengths sums to at most 128; some device holds a single sequence of exactly 128 tokens, and some slots are empty (length 0).
All inputs are finite; a program needn't handle non-finite values.
Results may differ from a plain program's by a relative error of at most 0.012.
Values may be sent and summed in bfloat16 or wider, within the bound.
No kernel may reach another device: no remote copies, remote signals or barrier semaphores. Data moves between devices by JAX's collectives and lax.ppermute only.
A program may use at most 256 MiB of HBM per device.

v0:
```python
import math
import jax
import jax.numpy as jnp
from jax import lax
from jax.sharding import PartitionSpec as P

HD = 64
ROT = 16
EPS = 1e-05
NEG = -1e30
CONTRACT_ROWS = (((0,), (0,)), ((), ()))
CONTRACT_COLS = (((1,), (1,)), ((), ()))


def block_terms(lengths_row, rows_tok):
    ends = jnp.cumsum(lengths_row)
    place = jnp.arange(rows_tok, dtype=jnp.int32)
    segment = jnp.sum((place[:, None] >= ends[None, :]).astype(jnp.int32), axis=1)
    starts = jnp.concatenate([ends - lengths_row, ends[-1:]])
    labels = jnp.arange(starts.shape[0], dtype=jnp.int32)
    begin = jnp.sum(jnp.where(segment[:, None] == labels[None, :], starts[None, :], 0), axis=1)
    position = (place - begin).astype(jnp.float32)
    valid = segment < lengths_row.shape[0]
    label_tok = jnp.where(valid, segment, lengths_row.shape[0] + place)
    allowed = (label_tok[:, None] == label_tok[None, :]) & (place[None, :] <= place[:, None])
    return (position, valid, allowed)


def angles(position):
    half = ROT // 2
    freq = jnp.exp(jnp.arange(half, dtype=jnp.float32) * (-2.0 * math.log(10000.0) / ROT))
    turn = position[:, None] * freq[None, :]
    return (jnp.cos(turn), jnp.sin(turn))


def rotate(heads_in, cosine, sine):
    half = ROT // 2
    first = heads_in[..., :half]
    second = heads_in[..., half:ROT]
    cos_b = cosine[:, None, :]
    sin_b = sine[:, None, :]
    return jnp.concatenate(
        [first * cos_b - second * sin_b, second * cos_b + first * sin_b, heads_in[..., ROT:]],
        axis=-1,
    )


def alternate(first, second, shards):
    rows_tok = first.shape[0]
    joined = jnp.concatenate(
        [first.reshape(rows_tok, shards, -1), second.reshape(rows_tok, shards, -1)], axis=2
    )
    return joined.reshape(rows_tok, -1)


def separate(joined, shards, split_at):
    rows_tok = joined.shape[0]
    blocks = joined.reshape(rows_tok, shards, -1)
    return (
        blocks[:, :, :split_at].reshape(rows_tok, -1),
        blocks[:, :, split_at:].reshape(rows_tok, -1),
    )


def on_device(
    tokens, ln_gain, ln_shift, w_qkv, b_qkv, w_out, w_gate, w_up, w_down, grad_out, seq_lengths
):
    shards = lax.axis_size(("dp", "fsdp"))
    rows_tok, width = tokens.shape
    heads = width // HD
    inner = w_gate.shape[1]
    own_rows = w_qkv.shape[0]
    position, valid, allowed = block_terms(seq_lengths[0], rows_tok)
    cosine, sine = angles(position)
    keep_row = valid.astype(jnp.float32)[:, None]
    widened = tokens.astype(jnp.float32)
    centered = widened - jnp.mean(widened, axis=1, keepdims=True)
    inv_std = lax.rsqrt(jnp.mean(centered * centered, axis=1, keepdims=True) + EPS)
    scaled = centered * inv_std
    normed = (scaled * ln_gain + ln_shift).astype(jnp.bfloat16)
    mixer = jnp.concatenate([w_out, w_down], axis=0)
    pieces = (
        lax.all_gather(w_qkv, ("dp", "fsdp"), axis=0, tiled=True),
        lax.all_gather(w_gate, ("dp", "fsdp"), axis=0, tiled=True),
        lax.all_gather(w_up, ("dp", "fsdp"), axis=0, tiled=True),
    )
    columns = normed
    proj_qkv, proj_gate, proj_up = tuple(
        (jnp.dot(columns, piece, preferred_element_type=jnp.float32) for piece in pieces)
    )
    split_qkv = (proj_qkv + b_qkv).reshape(rows_tok, 3, heads, HD)
    query = rotate(split_qkv[:, 0], cosine, sine).astype(jnp.bfloat16)
    keys = rotate(split_qkv[:, 1], cosine, sine).astype(jnp.bfloat16)
    values = split_qkv[:, 2].astype(jnp.bfloat16)
    scores = jnp.einsum("qhd,khd->hqk", query, keys, preferred_element_type=jnp.float32) * 0.125
    scores = jnp.where(allowed[None], scores, NEG)
    peak = jnp.max(scores, axis=2, keepdims=True)
    lifted = jnp.exp(scores - peak)
    row_total = jnp.sum(lifted, axis=2, keepdims=True)
    probs = lifted / row_total
    log_total = peak + jnp.log(row_total)
    attended = jnp.einsum(
        "hqk,khd->qhd", probs.astype(jnp.bfloat16), values, preferred_element_type=jnp.float32
    )
    attended = attended.reshape(rows_tok, width).astype(jnp.bfloat16)
    sigma = jax.nn.sigmoid(proj_gate)
    activ = proj_gate * sigma
    hidden = (activ * proj_up).astype(jnp.bfloat16)
    joined = alternate(attended, hidden, shards)
    columns = joined
    branch_sum = jnp.dot(
        columns,
        lax.all_gather(mixer, ("dp", "fsdp"), axis=0, tiled=True),
        preferred_element_type=jnp.float32,
    )
    output = (widened + keep_row * branch_sum).astype(jnp.bfloat16)
    masked = (grad_out.astype(jnp.float32) * keep_row).astype(jnp.bfloat16)
    back_mix = lax.dot_general(
        masked,
        lax.all_gather(mixer, ("dp", "fsdp"), axis=0, tiled=True),
        CONTRACT_COLS,
        preferred_element_type=jnp.float32,
    )
    grad_att, grad_hid = separate(back_mix, shards, own_rows)
    grad_mixed = grad_att.astype(jnp.bfloat16).reshape(rows_tok, heads, HD)
    redo = jnp.einsum("qhd,khd->hqk", query, keys, preferred_element_type=jnp.float32) * 0.125
    redo = jnp.where(allowed[None], redo, NEG)
    probs_again = jnp.exp(redo - log_total)
    grad_probs = jnp.einsum("qhd,khd->hqk", grad_mixed, values, preferred_element_type=jnp.float32)
    inner_sum = jnp.sum(probs_again * grad_probs, axis=2, keepdims=True)
    grad_scores = (probs_again * (grad_probs - inner_sum)).astype(jnp.bfloat16)
    grad_query = (
        jnp.einsum("hqk,khd->qhd", grad_scores, keys, preferred_element_type=jnp.float32) * 0.125
    )
    grad_keys = (
        jnp.einsum("hqk,qhd->khd", grad_scores, query, preferred_element_type=jnp.float32) * 0.125
    )
    grad_values = jnp.einsum(
        "hqk,qhd->khd",
        probs_again.astype(jnp.bfloat16),
        grad_mixed,
        preferred_element_type=jnp.float32,
    )
    grad_proj = jnp.stack(
        [rotate(grad_query, cosine, -sine), rotate(grad_keys, cosine, -sine), grad_values], axis=1
    )
    grad_proj = grad_proj.reshape(rows_tok, 3 * width).astype(jnp.bfloat16)
    slope = sigma * (1.0 + proj_gate * (1.0 - sigma))
    grad_gate = (grad_hid * proj_up * slope).astype(jnp.bfloat16)
    grad_up = (grad_hid * activ).astype(jnp.bfloat16)
    pieces = lax.all_gather((w_qkv, w_gate, w_up), ("dp", "fsdp"), axis=0, tiled=True)
    first = lax.dot_general(grad_proj, pieces[0], CONTRACT_COLS, preferred_element_type=jnp.float32)
    second = lax.dot_general(
        grad_gate, pieces[1], CONTRACT_COLS, preferred_element_type=jnp.float32
    )
    third = lax.dot_general(grad_up, pieces[2], CONTRACT_COLS, preferred_element_type=jnp.float32)
    grad_norm = first + second + third
    gain_part = jnp.sum(grad_norm * scaled, axis=0)
    shift_part = jnp.sum(grad_norm, axis=0)
    bias_part = jnp.sum(grad_proj.astype(jnp.float32), axis=0).reshape(width, 3)
    lifted_grad = grad_norm * ln_gain
    grad_in = inv_std * (
        lifted_grad
        - jnp.mean(lifted_grad, axis=1, keepdims=True)
        - scaled * jnp.mean(lifted_grad * scaled, axis=1, keepdims=True)
    )
    grad_tokens = (grad_out.astype(jnp.float32) + grad_in).astype(jnp.bfloat16)
    stats = jnp.concatenate(
        [gain_part[:, None], shift_part[:, None], bias_part, jnp.zeros((width, 123), jnp.float32)],
        axis=1,
    )
    outer = lax.axis_size("fsdp")
    group_rows = own_rows * outer
    normed_cols, joined_cols = (
        lax.all_to_all(normed, "dp", split_axis=1, concat_axis=0, tiled=True),
        lax.all_to_all(joined, "dp", split_axis=1, concat_axis=0, tiled=True),
    )
    stat_parts = lax.all_to_all(jnp.transpose(stats), "dp", split_axis=1, concat_axis=0, tiled=True)
    stat_sum = jnp.transpose(jnp.sum(stat_parts.reshape(-1, stats.shape[1], group_rows), axis=0))
    pieces = (
        lax.all_gather(grad_proj, "dp", axis=0, tiled=True),
        lax.all_gather(grad_gate, "dp", axis=0, tiled=True),
        lax.all_gather(grad_up, "dp", axis=0, tiled=True),
        lax.all_gather(masked, "dp", axis=0, tiled=True),
    )
    blocks = [
        lax.dot_general(normed_cols, piece, CONTRACT_ROWS, preferred_element_type=jnp.float32)
        for piece in pieces[:3]
    ]
    mixed_part = lax.dot_general(
        joined_cols, pieces[3], CONTRACT_ROWS, preferred_element_type=jnp.float32
    )
    input_part = jnp.concatenate(blocks, axis=1)
    input_part = jnp.concatenate([input_part, stat_sum], axis=1)
    input_sum, mixer_sum = (
        lax.psum_scatter(
            input_part.astype(jnp.bfloat16), "fsdp", scatter_dimension=0, tiled=True
        ).astype(jnp.float32),
        lax.psum_scatter(
            mixed_part.astype(jnp.bfloat16), "fsdp", scatter_dimension=0, tiled=True
        ).astype(jnp.float32),
    )
    qkv_cols = 3 * width
    grad_w_qkv = input_sum[:, :qkv_cols]
    grad_w_gate = input_sum[:, qkv_cols : qkv_cols + inner]
    grad_w_up = input_sum[:, qkv_cols + inner : qkv_cols + 2 * inner]
    tail_cols = input_sum[:, qkv_cols + 2 * inner :]
    grad_gain = tail_cols[:, 0]
    grad_shift = tail_cols[:, 1]
    grad_bias = tail_cols[:, 2:5].reshape(-1)
    grad_w_out = mixer_sum[:own_rows]
    grad_w_down = mixer_sum[own_rows:]
    return (
        output,
        grad_tokens,
        grad_w_qkv,
        grad_w_out,
        grad_w_gate,
        grad_w_up,
        grad_w_down,
        grad_gain,
        grad_shift,
        grad_bias,
    )


def solution(mesh):
    placed = (
        P(("dp", "fsdp"), None),
        P(),
        P(),
        P(("dp", "fsdp"), None),
        P(),
        P(("dp", "fsdp"), None),
        P(("dp", "fsdp"), None),
        P(("dp", "fsdp"), None),
        P(("dp", "fsdp"), None),
        P(("dp", "fsdp"), None),
        P(("dp", "fsdp"), None),
    )
    return jax.shard_map(
        on_device,
        mesh=mesh,
        in_specs=placed,
        out_specs=(
            P(("dp", "fsdp"), None),
            P(("dp", "fsdp"), None),
            P(("dp", "fsdp"), None),
            P(("dp", "fsdp"), None),
            P(("dp", "fsdp"), None),
            P(("dp", "fsdp"), None),
            P(("dp", "fsdp"), None),
            P(("dp", "fsdp")),
            P(("dp", "fsdp")),
            P(("dp", "fsdp")),
        ),
        check_vma=False,
    )
```

profile of v0, /device:TPU:0, one launch (start us, length us, event | category | flops | bytes accessed | tf_op | source)
XLA Modules:
  0.0 1287.0 jit_solution(11946301939778246751)
XLA Ops:
  13.9 144.3 %all-gather.13.cloned.1.call-done = bf16[2048,5632]{1,0:T(8,128)(2,1)} async-done(((bf16[64,5632]{1,0:T(8,128)(2,1)}), bf16[2048,5632]{1,0:T(8,128)(2,1)}) %all-gather.13.cloned.1.call-update) | async-done | bytes 23068688 | tf_op jit(solution)/shard_map/all_gather | solution.py:85
  158.2 12.3 fusion.36
  170.5 174.2 %all-gather.15.cloned.1.call-done = bf16[7680,2048]{1,0:T(8,128)(2,1)} async-done(((bf16[240,2048]{1,0:T(8,128)(2,1)}), bf16[7680,2048]{1,0:T(8,128)(2,1)}) %all-gather.15.cloned.1.call-update) | async-done | bytes 31457296 | tf_op jit(solution)/shard_map/all_gather | solution.py:113
  344.7 14.4 %fusion.37 = f32[128,7680]{0,1:T(8,128)S(1)} fusion(bf16[128,2048]{1,0:T(8,128)(2,1)S(1)} %copy-done.8, bf16[7680,2048]{1,0:T(8,128)(2,1)} %all-gather.15.cloned.1.call-done), kind=kOutput, calls=%fused_computation.107 | convolution fusion | flops 4026531840 | bytes 35913728 | tf_op jit(solution)/shard_map/dot_general | solution.py:118
  361.9 3.4 copy.50
  365.3 125.1 %all-gather.11.cloned.1.call-done = bf16[2048,5632]{1,0:T(8,128)(2,1)} async-done(((bf16[64,5632]{1,0:T(8,128)(2,1)}), bf16[2048,5632]{1,0:T(8,128)(2,1)}) %all-gather.11.cloned.1.call-update) | async-done | bytes 23068688 | tf_op jit(solution)/shard_map/all_gather | solution.py:84
  490.4 15.8 %multiply_convert_fusion = (bf16[128,5632]{1,0:T(8,128)(2,1)}, bf16[128,5632]{1,0:T(8,128)(2,1)}, bf16[128,5632]{1,0:T(8,128)(2,1)}) fusion(f32[128,5632]{1,0:T(8,128)} %copy.50, f32[128,5632]{1,0:T(8,128)} %fusion.36, bf16[128,2048]{1,0:T(8,128)(2,1)S(1)} %fusion.15, bf16[2048,5632]{1,0:T(8,128)(2,1)} %all-gather.11.cloned.1.call-done), kind=kOutput, calls=%fused_computation.8 | convolution fusion | flops 2963603456 | bytes 33685504 | tf_op jit(solution)/shard_map/dot_general | solution.py:89
  509.1 136.8 %all-gather.9.cloned.1.call-done = bf16[2048,6144]{1,0:T(8,128)(2,1)} async-done(((bf16[64,6144]{1,0:T(8,128)(2,1)}), bf16[2048,6144]{1,0:T(8,128)(2,1)}) %all-gather.9.cloned.1.call-update) | async-done | bytes 25165840 | tf_op jit(solution)/shard_map/all_gather | solution.py:83
  645.9 13.5 %convolution_add_fusion = f32[128,6144]{1,0:T(8,128)} fusion(bf16[128,2048]{1,0:T(8,128)(2,1)S(1)} %fusion.15, bf16[2048,6144]{1,0:T(8,128)(2,1)} %all-gather.9.cloned.1.call-done, f32[6144]{0:T(1024)S(1)} %copy-done.15), kind=kOutput, calls=%fused_computation.5 | convolution fusion | flops 3222011904 | bytes 28860416 | tf_op jit(solution)/shard_map/dot_general | solution.py:89
  659.5 3.6 copy.43
  674.0 2.5 fusion.13
  679.8 3.6 all-to-all-start.2
  683.7 83.4 %all-to-all-done.2 = bf16[128,4,1920]{0,2,1:T(8,128)(2,1)S(1)} async-done(((bf16[128,4,1920]{0,2,1:T(8,128)(2,1)}), bf16[128,4,1920]{0,2,1:T(8,128)(2,1)S(1)}, u32[]{:S(2)}, u32[]{:S(2)}) %all-to-all-start.2) | async-done | bytes 1966112 | tf_op jit(solution)/shard_map/all_to_all | solution.py:176
  769.6 9.7 convolution_convert_fusion.3
  780.7 14.2 %fusion.38 = f32[128,2048]{1,0:T(8,128)} fusion(bf16[128,6144]{0,1:T(8,128)(2,1)S(1)} %bitcast.81, bf16[2048,6144]{1,0:T(8,128)(2,1)} %all-gather.9.cloned.1.call-done), kind=kOutput, calls=%fused_computation.108 | convolution fusion | flops 3221225472 | bytes 27787264 | tf_op jit(solution)/shard_map/dot_general | solution.py:152
  794.8 12.5 convolution_add_fusion.2
  807.3 13.6 %fusion.19 = (f32[2048]{0:T(1024)S(1)}, f32[128]{0:T(128)S(1)}, f32[128]{0:T(128)S(1)}, f32[2048]{0:T(1024)S(1)}, f32[128,2048]{1,0:T(8,128)}) fusion(bf16[128,2048]{1,0:T(8,128)(2,1)S(1)} %copy-done.6, f32[128]{0:T(128)S(1)} %add_rsqrt_fusion, f32[128]{0:T(128)S(1)} %broadcast_multiply_fusion.2, f32[2048]{0:T(1024)S(1)} %copy-done.14, ...), kind=kOutput, calls=%fused_computation.49 | convolution fusion | flops 2955669504 | bytes 27158528 | tf_op jit(solution)/shard_map/dot_general | solution.py:156
  823.7 2.8 maximum_maximum_fusion
  826.5 3.5 all-to-all-start.1
  830.9 50.9 %all-to-all-done.1 = f32[128,4,512]{0,2,1:T(8,128)S(1)} async-done(((f32[128,4,512]{0,2,1:T(8,128)}), f32[128,4,512]{0,2,1:T(8,128)S(1)}, u32[]{:S(2)}, u32[]{:S(2)}) %all-to-all-start.1) | async-done | bytes 1048608 | tf_op jit(solution)/shard_map/all_to_all | solution.py:178
  881.8 3.5 all-to-all-start
  885.4 27.3 %all-to-all-done = bf16[128,4,512]{2,0,1:T(8,128)(2,1)S(1)} async-done(((bf16[128,4,512]{2,0,1:T(8,128)(2,1)}), bf16[128,4,512]{2,0,1:T(8,128)(2,1)S(1)}, u32[]{:S(2)}, u32[]{:S(2)}) %all-to-all-start) | async-done | bytes 524320 | tf_op jit(solution)/shard_map/all_to_all | solution.py:175
  912.7 7.7 convolution_convert_fusion
  920.4 40.2 %all-gather.19.cloned.1.call-done = bf16[512,5632]{1,0:T(8,128)(2,1)} async-done(((bf16[128,5632]{1,0:T(8,128)(2,1)}), bf16[512,5632]{1,0:T(8,128)(2,1)}) %all-gather.19.cloned.1.call-update) | async-done | bytes 5767184 | tf_op jit(solution)/shard_map/all_gather | solution.py:182
  960.6 7.6 convolution_convert_fusion.1
  968.3 108.3 %all-gather.17.cloned.1.call-done = bf16[512,6144]{0,1:T(8,128)(2,1)} async-done(((bf16[128,6144]{0,1:T(8,128)(2,1)}), bf16[512,6144]{0,1:T(8,128)(2,1)}) %all-gather.17.cloned.1.call-update) | async-done | bytes 6291472 | tf_op jit(solution)/shard_map/all_gather | solution.py:181
  1076.5 8.4 convolution_convert_fusion.2
  1084.9 10.8 pad_maximum_fusion
  1098.4 16.9 %fusion.2 = bf16[128,2048]{1,0:T(8,128)(2,1)} fusion(bf16[128,7680]{0,1:T(8,128)(2,1)} %bitcast.10, bf16[7680,2048]{1,0:T(8,128)(2,1)} %all-gather.15.cloned.1.call-done, bf16[128,2048]{1,0:T(8,128)(2,1)S(1)} %copy-done.6, f32[128]{0:T(128)S(1)} %compare_convert_fusion), kind=kOutput, calls=%fused_computation.17 | convolution fusion | flops 4027580416 | bytes 34472448 | tf_op jit(solution)/shard_map/dot_general | solution.py:111
  1115.3 32.3 %reduce-scatter.5.cloned.1.call-done = bf16[240,2048]{1,0:T(8,128)(2,1)} async-done(((bf16[1920,2048]{1,0:T(8,128)(2,1)}), bf16[240,2048]{1,0:T(8,128)(2,1)}) %reduce-scatter.5.cloned.1.call-update) | async-done | bytes 983056 | tf_op jit(solution)/shard_map/reduce_scatter | solution.py:199
  1147.6 2.5 slice.137
  1150.9 122.3 %reduce-scatter.3.cloned.1.call-done = bf16[64,17536]{1,0:T(8,128)(2,1)} async-done(((bf16[512,17536]{1,0:T(8,128)(2,1)}), bf16[64,17536]{1,0:T(8,128)(2,1)}) %reduce-scatter.3.cloned.1.call-update) | async-done | bytes 2244624 | tf_op jit(solution)/shard_map/reduce_scatter | solution.py:196
  (115 shorter events, 44.2 us)
Async XLA Ops:
  7.2 4.5 copy-start.17
  7.2 4.7 copy-start.11
  7.2 151.0 %all-gather.13.cloned.1.call-start = ((), (), s32[]{:S(2)}) async-start(), calls=%async_computation.7 | async-start | bytes 23789568 | tf_op jit(solution)/shard_map/all_gather | solution.py:85
  7.9 5.0 copy-start.6
  7.9 336.8 %all-gather.15.cloned.1.call-start = ((), (), s32[]{:S(2)}) async-start(), calls=%async_computation.8 | async-start | bytes 32440320 | tf_op jit(solution)/shard_map/all_gather | solution.py:113
  10.3 3.2 copy-start.14
  10.3 3.2 copy-start.16
  10.3 480.1 %all-gather.11.cloned.1.call-start = ((), (), s32[]{:S(2)}) async-start(), calls=%async_computation.6 | async-start | bytes 23789568 | tf_op jit(solution)/shard_map/all_gather | solution.py:84
  11.0 634.9 %all-gather.9.cloned.1.call-start = ((), (), s32[]{:S(2)}) async-start(), calls=%async_computation.5 | async-start | bytes 25952256 | tf_op jit(solution)/shard_map/all_gather | solution.py:83
  11.6 758.0 %all-gather.23.cloned.1.call-start = ((), (), s32[]{:S(2)}) async-start(), calls=%async_computation.13 | async-start | bytes 2621440 | tf_op jit(solution)/shard_map/all_gather | solution.py:184
  12.9 899.8 %all-gather.21.cloned.1.call-start = ((), (), s32[]{:S(2)}) async-start(), calls=%async_computation.11 | async-start | bytes 7208960 | tf_op jit(solution)/shard_map/all_gather | solution.py:183
  13.9 330.9 %copy-start.8 = (bf16[128,2048]{1,0:T(8,128)(2,1)S(1)}, bf16[128,2048]{1,0:T(8,128)(2,1)}, u32[]{:S(2)}) copy-start(bf16[128,2048]{1,0:T(8,128)(2,1)} %fusion.21) | copy-start | bytes 1572868
  359.1 2.8 copy-start.3
  506.2 139.7 %copy-start.15 = (f32[6144]{0:T(1024)S(1)}, f32[6144]{0:T(1024)}, u32[]{:S(2)}) copy-start(f32[6144]{0:T(1024)} %param.15) | copy-start | bytes 73732
  506.2 454.4 %all-gather.19.cloned.1.call-start = ((), (), s32[]{:S(2)}) async-start(), calls=%async_computation.10 | async-start | bytes 7208960 | tf_op jit(solution)/shard_map/all_gather | solution.py:182
  507.0 569.5 %all-gather.17.cloned.1.call-start = ((), (), s32[]{:S(2)}) async-start(), calls=%async_computation.9 | async-start | bytes 7864320 | tf_op jit(solution)/shard_map/all_gather | solution.py:181
  664.9 2.1 copy-start.4
  676.5 1.9 copy-start.13
  679.8 87.4 %all-to-all-start.2 = ((bf16[128,4,1920]{0,2,1:T(8,128)(2,1)}), bf16[128,4,1920]{0,2,1:T(8,128)(2,1)S(1)}, u32[]{:S(2)}, u32[]{:S(2)}) async-start(bf16[128,4,1920]{0,2,1:T(8,128)(2,1)} %bitcast.28), calls=%async_computation.3 | async-start | bytes 3932160 | tf_op jit(solution)/shard_map/all_to_all | solution.py:176
  683.4 464.1 %reduce-scatter.5.cloned.1.call-start = ((), (), s32[]{:S(2)}) async-start(), calls=%async_computation.14 | async-start | bytes 8847360 | tf_op jit(solution)/shard_map/reduce_scatter | solution.py:199
  779.3 1.4 copy-start.2
  794.8 12.5 copy-start.7
  826.5 55.2 %all-to-all-start.1 = ((f32[128,4,512]{0,2,1:T(8,128)}), f32[128,4,512]{0,2,1:T(8,128)S(1)}, u32[]{:S(2)}, u32[]{:S(2)}) async-start(f32[128,4,512]{0,2,1:T(8,128)} %bitcast.26), calls=%async_computation.1 | async-start | bytes 2097152 | tf_op jit(solution)/shard_map/all_to_all | solution.py:178
  881.8 30.9 %all-to-all-start = ((bf16[128,4,512]{2,0,1:T(8,128)(2,1)}), bf16[128,4,512]{2,0,1:T(8,128)(2,1)S(1)}, u32[]{:S(2)}, u32[]{:S(2)}) async-start(bf16[128,4,512]{2,0,1:T(8,128)(2,1)} %bitcast.79), calls=%async_computation | async-start | bytes 1048576 | tf_op jit(solution)/shard_map/all_to_all | solution.py:175
  885.3 387.9 %reduce-scatter.3.cloned.1.call-start = ((), (), s32[]{:S(2)}) async-start(), calls=%async_computation.12 | async-start | bytes 20201472 | tf_op jit(solution)/shard_map/reduce_scatter | solution.py:196
  1076.5 8.4 copy-start
  1076.5 8.4 copy-start.1
  1095.7 1.2 copy-start.9
  1095.7 1.4 copy-start.12
  1147.6 2.5 copy-start.10
  1273.1 2.8 copy-start.5
Sparse Core Ops, SparseCore 0:
  10.9 147.2 all-gather.12
  161.7 182.9 all-gather.14
  347.6 142.7 all-gather.10
  493.1 152.7 all-gather.8
  647.9 57.1 all-gather.22
  707.2 120.0 all-gather.20
  829.4 131.1 all-gather.18
  962.8 113.6 all-gather.16
  1080.0 67.5 reduce-scatter.4
  1151.6 121.4 reduce-scatter.2
where the time goes:
time: 1300 us; the launch traced here: 1290 us
  waiting for transfers between devices  1050 us (81%)
  matrix products  154 us (12%)
  local copies, waits for them, and re-layouts  32 us (2%)
  other arithmetic  27.1 us (2%)
  between operations  14.9 us (1%)
    all_gather x1, waiting for transfers between devices, on_device(): lax.all_gather(mixer, ('dp', 'fsdp'), axis=0, tiled=True)  174 us
    all_gather x1, waiting for transfers between devices, on_device(): lax.all_gather(w_up, ('dp', 'fsdp'), axis=0, tiled=True)  144 us
    all_gather x1, waiting for transfers between devices, on_device(): lax.all_gather(w_qkv, ('dp', 'fsdp'), axis=0, tiled=True)  137 us
    all_gather x1, waiting for transfers between devices, on_device(): lax.all_gather(w_gate, ('dp', 'fsdp'), axis=0, tiled=True)  125 us
    reduce_scatter x1, waiting for transfers between devices, on_device(): lax.psum_scatter(input_part.astype(jnp.bfloat16), 'fsdp', scatter_dimensi...  122 us
    all_gather x1, waiting for transfers between devices, on_device(): lax.all_gather(grad_proj, 'dp', axis=0, tiled=True)  108 us
    all_to_all x1, waiting for transfers between devices, on_device(): lax.all_to_all(joined, 'dp', split_axis=1, concat_axis=0, tiled=True)  83.4 us
    all_to_all x1, waiting for transfers between devices, on_device(): lax.all_to_all(jnp.transpose(stats), 'dp', split_axis=1, concat_axis=0, t...  50.9 us
  transfers between devices with their start and end apart: 13, of which 11 were waited for; matrix products, arithmetic and copies ran while one was open for 16% of the time, Pallas kernels for 0%

commit v1 on v0

--- a/solution.py
+++ b/solution.py
@@ -10,6 +10,27 @@
 NEG = -1e30
 CONTRACT_ROWS = (((0,), (0,)), ((), ()))
 CONTRACT_COLS = (((1,), (1,)), ((), ()))
+
+
+def ring_gather(x, axis, dim):
+    length, index, rows = (lax.axis_size(axis), lax.axis_index(axis), x.shape[dim])
+    forward = [(i, (i + 1) % length) for i in range(length)]
+    left = [(i, (i - 1) % length) for i in range(length)]
+    out = jnp.zeros((*x.shape[:dim], length * rows, *x.shape[dim + 1 :]), x.dtype)
+    out = lax.dynamic_update_slice_in_dim(out, x, index * rows, axis=dim)
+    from_left = from_right = x
+    halfway = length // 2
+    for step in range(1, halfway + 1):
+        from_left = lax.ppermute(from_left, axis, forward)
+        out = lax.dynamic_update_slice_in_dim(
+            out, from_left, (index - step) % length * rows, axis=dim
+        )
+        if step < length - halfway:
+            from_right = lax.ppermute(from_right, axis, left)
+            out = lax.dynamic_update_slice_in_dim(
+                out, from_right, (index + step) % length * rows, axis=dim
+            )
+    return out
 
 
 def block_terms(lengths_row, rows_tok):
@@ -179,7 +200,7 @@
     stat_sum = jnp.transpose(jnp.sum(stat_parts.reshape(-1, stats.shape[1], group_rows), axis=0))
     pieces = (
         lax.all_gather(grad_proj, "dp", axis=0, tiled=True),
-        lax.all_gather(grad_gate, "dp", axis=0, tiled=True),
+        ring_gather(grad_gate, "dp", 0),
         lax.all_gather(grad_up, "dp", axis=0, tiled=True),
         lax.all_gather(masked, "dp", axis=0, tiled=True),
     )

time: 1300 us -> 1280 us (0.985)
  waiting for transfers between devices: 1050 us -> 973 us
  starting transfers between devices: 11.6 us -> 51.4 us
  local copies, waits for them, and re-layouts: 32 us -> 45.2 us
    all_gather x1, waiting for transfers between devices: 108 us -> 31.1 us  [on_device(): lax.all_gather(grad_proj, 'dp', axis=0, tiled=True)]
    all_gather x1 -> x0, waiting for transfers between devices: 40.2 us -> none  [on_device(): lax.all_gather(grad_gate, 'dp', axis=0, tiled=True)]
    ppermute x0 -> x3, waiting for transfers between devices: none -> 37.1 us  [the longest x1 37.1 us: ring_gather(): from_right = lax.ppermute(from_right, axis, left)]
    all_to_all x1, starting transfers between devices: 3.47 us -> 32.7 us  [on_device(): lax.all_to_all(normed, 'dp', split_axis=1, concat_axis=0, tiled=True)]
    all_to_all x1, waiting for transfers between devices: 27.3 us -> 52.9 us  [on_device(): lax.all_to_all(normed, 'dp', split_axis=1, concat_axis=0, tiled=True)]
    all_to_all x1, waiting for transfers between devices: 50.9 us -> 25.6 us  [on_device(): lax.all_to_all(jnp.transpose(stats), 'dp', split_axis=1, concat_axis=0, t...]
  transfers between devices with their start and end apart: 13 -> 15, of which waited for: 11 -> 11; matrix products, arithmetic and copies ran while one was open for 16% -> 17% of each run, Pallas kernels for 0% -> 0%
where the time goes in v1:
time: 1280 us; the launch traced here: 1270 us
  waiting for transfers between devices  973 us (76%)
  matrix products  152 us (12%)
  starting transfers between devices  51.4 us (4%)
  local copies, waits for them, and re-layouts  45.2 us (4%)
  other arithmetic  32.3 us (3%)
  between operations  14.5 us (1%)
    all_gather x1, waiting for transfers between devices, on_device(): lax.all_gather(mixer, ('dp', 'fsdp'), axis=0, tiled=True)  174 us
    all_gather x1, waiting for transfers between devices, on_device(): lax.all_gather(w_up, ('dp', 'fsdp'), axis=0, tiled=True)  144 us
    all_gather x1, waiting for transfers between devices, on_device(): lax.all_gather(w_qkv, ('dp', 'fsdp'), axis=0, tiled=True)  137 us
    all_gather x1, waiting for transfers between devices, on_device(): lax.all_gather(w_gate, ('dp', 'fsdp'), axis=0, tiled=True)  125 us
    reduce_scatter x1, waiting for transfers between devices, on_device(): lax.psum_scatter(input_part.astype(jnp.bfloat16), 'fsdp', scatter_dimensi...  122 us
    all_to_all x1, waiting for transfers between devices, on_device(): lax.all_to_all(joined, 'dp', split_axis=1, concat_axis=0, tiled=True)  87.9 us
    all_to_all x1, waiting for transfers between devices, on_device(): lax.all_to_all(normed, 'dp', split_axis=1, concat_axis=0, tiled=True)  52.9 us
    dot_general x3, matrix products, on_device(): jnp.dot(columns, piece, preferred_element_type=jnp.float32)  41.9 us
  transfers between devices with their start and end apart: 15, of which 11 were waited for; matrix products, arithmetic and copies ran while one was open for 17% of the time, Pallas kernels for 0%

profile of v1, /device:TPU:0, one launch (start us, length us, event | category | flops | bytes accessed | tf_op | source)
XLA Modules:
  0.0 1268.1 jit_solution(1918029391175718902)
XLA Ops:
  13.9 144.3 %all-gather.12.cloned.1.call-done = bf16[2048,5632]{1,0:T(8,128)(2,1)} async-done(((bf16[64,5632]{1,0:T(8,128)(2,1)}), bf16[2048,5632]{1,0:T(8,128)(2,1)}) %all-gather.12.cloned.1.call-update) | async-done | bytes 23068688 | tf_op jit(solution)/shard_map/all_gather | solution.py:106
  158.2 12.3 fusion.36
  170.5 174.2 %all-gather.14.cloned.1.call-done = bf16[7680,2048]{1,0:T(8,128)(2,1)} async-done(((bf16[240,2048]{1,0:T(8,128)(2,1)}), bf16[7680,2048]{1,0:T(8,128)(2,1)}) %all-gather.14.cloned.1.call-update) | async-done | bytes 31457296 | tf_op jit(solution)/shard_map/all_gather | solution.py:134
  344.7 14.4 %fusion.37 = f32[128,7680]{0,1:T(8,128)S(1)} fusion(bf16[128,2048]{1,0:T(8,128)(2,1)S(1)} %copy-done.10, bf16[7680,2048]{1,0:T(8,128)(2,1)} %all-gather.14.cloned.1.call-done), kind=kOutput, calls=%fused_computation.111 | convolution fusion | flops 4026531840 | bytes 35913728 | tf_op jit(solution)/shard_map/dot_general | solution.py:139
  362.0 3.4 copy.50
  365.4 125.0 %all-gather.10.cloned.1.call-done = bf16[2048,5632]{1,0:T(8,128)(2,1)} async-done(((bf16[64,5632]{1,0:T(8,128)(2,1)}), bf16[2048,5632]{1,0:T(8,128)(2,1)}) %all-gather.10.cloned.1.call-update) | async-done | bytes 23068688 | tf_op jit(solution)/shard_map/all_gather | solution.py:105
  490.4 16.0 %multiply_convert_fusion = (bf16[128,5632]{1,0:T(8,128)(2,1)}, bf16[128,5632]{1,0:T(8,128)(2,1)}, f32[128,5632]{1,0:T(8,128)}) fusion(f32[128,5632]{1,0:T(8,128)} %copy.50, f32[128,5632]{1,0:T(8,128)} %fusion.36, bf16[128,2048]{1,0:T(8,128)(2,1)S(1)} %fusion.15, bf16[2048,5632]{1,0:T(8,128)(2,1)} %all-gather.10.cloned.1.call-done), kind=kOutput, calls=%fused_computation.8 | convolution fusion | flops 2958557184 | bytes 35127296 | tf_op jit(solution)/shard_map/dot_general | solution.py:110
  508.5 137.5 %all-gather.8.cloned.1.call-done = bf16[2048,6144]{1,0:T(8,128)(2,1)} async-done(((bf16[64,6144]{1,0:T(8,128)(2,1)}), bf16[2048,6144]{1,0:T(8,128)(2,1)}) %all-gather.8.cloned.1.call-update) | async-done | bytes 25165840 | tf_op jit(solution)/shard_map/all_gather | solution.py:104
  646.0 13.6 %convolution_add_fusion = f32[128,6144]{1,0:T(8,128)} fusion(bf16[128,2048]{1,0:T(8,128)(2,1)S(1)} %fusion.15, bf16[2048,6144]{1,0:T(8,128)(2,1)} %all-gather.8.cloned.1.call-done, f32[6144]{0:T(1024)S(1)} %copy-done.16), kind=kOutput, calls=%fused_computation.5 | convolution fusion | flops 3222011904 | bytes 28860416 | tf_op jit(solution)/shard_map/dot_general | solution.py:110
  659.6 3.6 copy.43
  680.0 4.4 all-to-all-start.2
  689.2 4.9 constant_dynamic-update-slice_fusion.3
  696.2 14.2 %fusion.38 = f32[128,2048]{1,0:T(8,128)} fusion(bf16[128,6144]{0,1:T(8,128)(2,1)S(1)} %bitcast.81, bf16[2048,6144]{1,0:T(8,128)(2,1)} %all-gather.8.cloned.1.call-done), kind=kOutput, calls=%fused_computation.112 | convolution fusion | flops 3221225472 | bytes 27787264 | tf_op jit(solution)/shard_map/dot_general | solution.py:173
  710.4 87.9 %all-to-all-done.2 = bf16[128,4,1920]{0,2,1:T(8,128)(2,1)} async-done(((bf16[128,4,1920]{0,2,1:T(8,128)(2,1)}), bf16[128,4,1920]{0,2,1:T(8,128)(2,1)}, u32[]{:S(2)}, u32[]{:S(2)}) %all-to-all-start.2) | async-done | bytes 1966112 | tf_op jit(solution)/shard_map/all_to_all | solution.py:197
  801.1 7.9 convolution_convert_fusion.3
  809.0 12.5 convolution_add_fusion.2
  821.5 13.5 %fusion.19 = (f32[2048]{0:T(1024)S(1)}, f32[128]{0:T(128)S(1)}, f32[128]{0:T(128)S(1)}, f32[2048]{0:T(1024)S(1)}, f32[128,2048]{1,0:T(8,128)}) fusion(bf16[128,2048]{1,0:T(8,128)(2,1)S(1)} %copy-done.6, f32[128]{0:T(128)S(1)} %add_rsqrt_fusion, f32[128]{0:T(128)S(1)} %broadcast_multiply_fusion.2, f32[2048]{0:T(1024)S(1)} %copy-done.15, ...), kind=kOutput, calls=%fused_computation.49 | convolution fusion | flops 2955669504 | bytes 27158528 | tf_op jit(solution)/shard_map/dot_general | solution.py:177
  840.6 3.5 all-to-all-start.1
  844.1 3.8 collective-permute-start.1
  847.9 3.9 collective-permute-start.2
  855.2 25.6 %all-to-all-done.1 = f32[128,4,512]{0,2,1:T(8,128)S(1)} async-done(((f32[128,4,512]{0,2,1:T(8,128)}), f32[128,4,512]{0,2,1:T(8,128)S(1)}, u32[]{:S(2)}, u32[]{:S(2)}) %all-to-all-start.1) | async-done | bytes 1048608 | tf_op jit(solution)/shard_map/all_to_all | solution.py:199
  880.8 32.7 %all-to-all-start = ((bf16[128,4,512]{2,0,1:T(8,128)(2,1)}), bf16[128,4,512]{2,0,1:T(8,128)(2,1)S(1)}, u32[]{:S(2)}, u32[]{:S(2)}) async-start(bf16[128,4,512]{2,0,1:T(8,128)(2,1)} %bitcast.79), calls=%async_computation | async-start | bytes 1048576 | tf_op jit(solution)/shard_map/all_to_all | solution.py:196
  913.7 37.1 %collective-permute-done.1 = bf16[128,5632]{1,0:T(8,128)(2,1)} collective-permute-done((bf16[128,5632]{1,0:T(8,128)(2,1)}, bf16[128,5632]{1,0:T(8,128)(2,1)}, u32[]{:S(2)}, u32[]{:S(2)}) %collective-permute-start.1) | collective-permute-done | bytes 1441824 | tf_op jit(solution)/shard_map/ppermute | solution.py:29
  956.0 52.9 %all-to-all-done = bf16[128,4,512]{2,0,1:T(8,128)(2,1)S(1)} async-done(((bf16[128,4,512]{2,0,1:T(8,128)(2,1)}), bf16[128,4,512]{2,0,1:T(8,128)(2,1)S(1)}, u32[]{:S(2)}, u32[]{:S(2)}) %all-to-all-start) | async-done | bytes 524320 | tf_op jit(solution)/shard_map/all_to_all | solution.py:196
  1008.9 7.6 convolution_convert_fusion.1
  1016.5 7.6 convolution_convert_fusion
  1024.2 31.1 %all-gather.16.cloned.1.call-done = bf16[512,6144]{0,1:T(8,128)(2,1)} async-done(((bf16[128,6144]{0,1:T(8,128)(2,1)}), bf16[512,6144]{0,1:T(8,128)(2,1)}) %all-gather.16.cloned.1.call-update) | async-done | bytes 6291472 | tf_op jit(solution)/shard_map/all_gather | solution.py:202
  1055.2 8.3 convolution_convert_fusion.2
  1063.6 11.2 pad_maximum_fusion
  1077.5 16.9 %fusion.2 = bf16[128,2048]{1,0:T(8,128)(2,1)} fusion(bf16[128,7680]{0,1:T(8,128)(2,1)} %bitcast.10, bf16[7680,2048]{1,0:T(8,128)(2,1)} %all-gather.14.cloned.1.call-done, bf16[128,2048]{1,0:T(8,128)(2,1)S(1)} %copy-done.6, f32[128]{0:T(128)S(1)} %compare_convert_fusion), kind=kOutput, calls=%fused_computation.17 | convolution fusion | flops 4027580416 | bytes 34472448 | tf_op jit(solution)/shard_map/dot_general | solution.py:132
  1094.4 33.8 %reduce-scatter.5.cloned.1.call-done = bf16[240,2048]{1,0:T(8,128)(2,1)} async-done(((bf16[1920,2048]{1,0:T(8,128)(2,1)}), bf16[240,2048]{1,0:T(8,128)(2,1)}) %reduce-scatter.5.cloned.1.call-update) | async-done | bytes 983056 | tf_op jit(solution)/shard_map/reduce_scatter | solution.py:220
  1132.4 121.6 %reduce-scatter.3.cloned.1.call-done = bf16[64,17536]{1,0:T(8,128)(2,1)} async-done(((bf16[512,17536]{1,0:T(8,128)(2,1)}), bf16[64,17536]{1,0:T(8,128)(2,1)}) %reduce-scatter.3.cloned.1.call-update) | async-done | bytes 2244624 | tf_op jit(solution)/shard_map/reduce_scatter | solution.py:217
  (125 shorter events, 66.5 us)
Async XLA Ops:
  7.2 4.5 copy-start.18
  7.2 4.7 copy-start.12
  7.2 151.0 %all-gather.12.cloned.1.call-start = ((), (), s32[]{:S(2)}) async-start(), calls=%async_computation.7 | async-start | bytes 23789568 | tf_op jit(solution)/shard_map/all_gather | solution.py:106
  7.9 5.0 copy-start.6
  7.9 336.8 %all-gather.14.cloned.1.call-start = ((), (), s32[]{:S(2)}) async-start(), calls=%async_computation.8 | async-start | bytes 32440320 | tf_op jit(solution)/shard_map/all_gather | solution.py:134
  10.3 3.2 copy-start.15
  10.3 3.2 copy-start.17
  10.3 480.1 %all-gather.10.cloned.1.call-start = ((), (), s32[]{:S(2)}) async-start(), calls=%async_computation.6 | async-start | bytes 23789568 | tf_op jit(solution)/shard_map/all_gather | solution.py:105
  11.0 635.0 %all-gather.8.cloned.1.call-start = ((), (), s32[]{:S(2)}) async-start(), calls=%async_computation.5 | async-start | bytes 25952256 | tf_op jit(solution)/shard_map/all_gather | solution.py:104
  11.6 789.5 %all-gather.20.cloned.1.call-start = ((), (), s32[]{:S(2)}) async-start(), calls=%async_computation.12 | async-start | bytes 2621440 | tf_op jit(solution)/shard_map/all_gather | solution.py:205
  12.9 1003.6 %all-gather.18.cloned.1.call-start = ((), (), s32[]{:S(2)}) async-start(), calls=%async_computation.10 | async-start | bytes 7208960 | tf_op jit(solution)/shard_map/all_gather | solution.py:204
  13.9 330.9 %copy-start.10 = (bf16[128,2048]{1,0:T(8,128)(2,1)S(1)}, bf16[128,2048]{1,0:T(8,128)(2,1)}, u32[]{:S(2)}) copy-start(bf16[128,2048]{1,0:T(8,128)(2,1)} %fusion.21) | copy-start | bytes 1572868
  359.1 2.8 copy-start.3
  365.4 280.6 %copy-start.16 = (f32[6144]{0:T(1024)S(1)}, f32[6144]{0:T(1024)}, u32[]{:S(2)}) copy-start(f32[6144]{0:T(1024)} %param.15) | copy-start | bytes 73732
  506.4 548.9 %all-gather.16.cloned.1.call-start = ((), (), s32[]{:S(2)}) async-start(), calls=%async_computation.9 | async-start | bytes 7864320 | tf_op jit(solution)/shard_map/all_gather | solution.py:202
  665.0 2.1 copy-start.4
  676.7 1.9 copy-start.14
  680.0 118.3 %all-to-all-start.2 = ((bf16[128,4,1920]{0,2,1:T(8,128)(2,1)}), bf16[128,4,1920]{0,2,1:T(8,128)(2,1)}, u32[]{:S(2)}, u32[]{:S(2)}) async-start(bf16[128,4,1920]{0,2,1:T(8,128)(2,1)} %bitcast.28), calls=%async_computation.3 | async-start | bytes 3932160 | tf_op jit(solution)/shard_map/all_to_all | solution.py:197
  684.4 443.9 %reduce-scatter.5.cloned.1.call-start = ((), (), s32[]{:S(2)}) async-start(), calls=%async_computation.13 | async-start | bytes 8847360 | tf_op jit(solution)/shard_map/reduce_scatter | solution.py:220
  684.4 3.3 copy-start.7
  684.5 4.8 copy-start.8
  689.2 7.0 copy-start.2
  694.1 153.8 %collective-permute-start = (bf16[128,5632]{1,0:T(8,128)(2,1)}, bf16[128,5632]{1,0:T(8,128)(2,1)}, u32[]{:S(2)}, u32[]{:S(2)}) collective-permute-start(bf16[128,5632]{1,0:T(8,128)(2,1)} %get-tuple-element.17), channel_id=1, source_target_pairs={{0,8},{8,16},{16,24},{24,0},{1,9},{9,17},{17,25},{25,1},{2,10},{10... | collective-permute-start | bytes 4325384 | tf_op jit(solution)/shard_map/ppermute | solution.py:24
  809.0 12.5 copy-start.9
  840.6 40.2 %all-to-all-start.1 = ((f32[128,4,512]{0,2,1:T(8,128)}), f32[128,4,512]{0,2,1:T(8,128)S(1)}, u32[]{:S(2)}, u32[]{:S(2)}) async-start(f32[128,4,512]{0,2,1:T(8,128)} %bitcast.26), calls=%async_computation.1 | async-start | bytes 2097152 | tf_op jit(solution)/shard_map/all_to_all | solution.py:199
  844.1 106.7 %collective-permute-start.1 = (bf16[128,5632]{1,0:T(8,128)(2,1)}, bf16[128,5632]{1,0:T(8,128)(2,1)}, u32[]{:S(2)}, u32[]{:S(2)}) collective-permute-start(bf16[128,5632]{1,0:T(8,128)(2,1)} %get-tuple-element.17), channel_id=1, source_target_pairs={{0,24},{8,0},{16,8},{24,16},{1,25},{9,1},{17,9},{25,17},{2,26},{10... | collective-permute-start | bytes 4325384 | tf_op jit(solution)/shard_map/ppermute | solution.py:29
  847.9 105.5 %collective-permute-start.2 = (bf16[128,5632]{1,0:T(8,128)(2,1)}, bf16[128,5632]{1,0:T(8,128)(2,1)}, u32[]{:S(2)}, u32[]{:S(2)}) collective-permute-start(bf16[128,5632]{1,0:T(8,128)(2,1)} %collective-permute-done), channel_id=1, source_target_pairs={{0,8},{8,16},{16,24},{24,0},{1,9},{9,17},{17,25},{25,1},{2,10},{10... | collective-permute-start | bytes 4325384 | tf_op jit(solution)/shard_map/ppermute | solution.py:24
  880.8 128.1 %all-to-all-start = ((bf16[128,4,512]{2,0,1:T(8,128)(2,1)}), bf16[128,4,512]{2,0,1:T(8,128)(2,1)S(1)}, u32[]{:S(2)}, u32[]{:S(2)}) async-start(bf16[128,4,512]{2,0,1:T(8,128)(2,1)} %bitcast.79), calls=%async_computation | async-start | bytes 1048576 | tf_op jit(solution)/shard_map/all_to_all | solution.py:196
  913.5 340.5 %reduce-scatter.3.cloned.1.call-start = ((), (), s32[]{:S(2)}) async-start(), calls=%async_computation.11 | async-start | bytes 20201472 | tf_op jit(solution)/shard_map/reduce_scatter | solution.py:217
  1055.2 8.3 copy-start
  1055.2 8.3 copy-start.1
  1255.5 2.8 copy-start.5
  (2 other events, 2.7 us)
Sparse Core Ops, SparseCore 0:
  10.9 147.2 all-gather.11
  161.7 182.9 all-gather.13
  347.6 142.7 all-gather.9
  493.1 152.8 all-gather.7
  648.0 56.6 all-gather.19
  706.7 175.2 all-gather.17
  884.1 171.0 all-gather.15
  1058.7 69.5 reduce-scatter.4
  1132.4 121.4 reduce-scatter.2
